TPU v7x, 32 devices: a whole 2x2x4 slice. The times are simulated.
32 devices in a mesh: seq: 8 (over z, y), mp: 4 (over x, core).
Axes of the slice: x: 2, y: 2, z: 4, core: 2. Of those that a mesh axis runs over, the one named last changes fastest.
Arguments:
- block_input: bfloat16 [1, 1280, 2560], P(None, 'seq'), may hold values from -6 to 6
- mix_gain: float32 [2560], replicated, may hold values from 0.5 to 1.5
- x_weight: bfloat16 [2560, 2560], P(None, 'mp'), may hold values from -0.125 to 0.125
- y_weight: bfloat16 [2560, 2560], P(None, 'mp'), may hold values from -0.125 to 0.125
- conv_weight: float32 [4, 2560], P(None, 'mp'), may hold values from -3 to 3
- conv_bias: float32 [2560], P('mp'), may hold values from -3 to 3
- input_gate: bfloat16 [256, 2560], P(None, 'mp'), may hold values from -0.375 to 0.375
- decay_gate: bfloat16 [256, 2560], P(None, 'mp'), may hold values from -0.375 to 0.375
- decay_param: float32 [2560], P('mp'), may hold values from -13 to -5
- out_weight: bfloat16 [2560, 2560], P('mp'), may hold values from -0.125 to 0.125
- ffn_gain: float32 [2560], replicated, may hold values from 0.5 to 1.5
- gate_weight: bfloat16 [2560, 7680], P(None, 'mp'), may hold values from -0.125 to 0.125
- up_weight: bfloat16 [2560, 7680], P(None, 'mp'), may hold values from -0.125 to 0.125
- down_weight: bfloat16 [7680, 2560], P('mp'), may hold values from -0.0625 to 0.0625
- out_cotangent: bfloat16 [1, 1280, 2560], P(None, 'seq'), may hold values from -6 to 6
Outputs:
- block_output: bfloat16 [1, 1280, 2560], P(None, 'seq')
- input_grad: bfloat16 [1, 1280, 2560], P(None, 'seq')
- mix_gain_grad: float32 [2560], P('seq')
- x_weight_grad: float32 [2560, 2560], P('seq', 'mp')
- y_weight_grad: float32 [2560, 2560], P('seq', 'mp')
- conv_weight_grad: float32 [4, 2560], P(None, ('mp', 'seq'))
- conv_bias_grad: float32 [2560], P(('mp', 'seq'))
- input_gate_grad: float32 [256, 2560], P('seq', 'mp')
- decay_gate_grad: float32 [256, 2560], P('seq', 'mp')
- decay_param_grad: float32 [2560], P(('mp', 'seq'))
- out_weight_grad: float32 [2560, 2560], P('mp', 'seq')
- ffn_gain_grad: float32 [2560], P('seq')
- gate_weight_grad: float32 [2560, 7680], P('seq', 'mp')
- up_weight_grad: float32 [2560, 7680], P('seq', 'mp')
- down_weight_grad: float32 [7680, 2560], P('mp', 'seq')
All inputs are finite; a program needn't handle non-finite values.
Results may differ from a plain program's by a relative error of at most 0.009.
Values may be sent and summed in bfloat16 or wider, within the bound.
No kernel may reach another device: no remote copies, remote signals or barrier semaphores. Data moves between devices by JAX's collectives and lax.ppermute only.
A program may use at most 320 MiB of HBM per device.

v0:
```python
import jax
import jax.numpy as jnp
from jax import lax
from jax.sharding import PartitionSpec as P

EPS = 1e-06


def passed_along(shard, axis, by):
    size = lax.axis_size(axis)
    pairs = [(i, i + by) for i in range(size) if 0 <= i + by < size]
    return lax.ppermute(shard, axis, pairs)


def carried_in(value, axis, join, neutral, backward):
    count, mine = (lax.axis_size(axis), lax.axis_index(axis))
    pieces = jax.tree.map(lambda part: lax.all_gather(part, axis), value)
    if backward:
        pieces = jax.tree.map(lambda part: part[::-1], pieces)
        mine = count - 1 - mine
    so_far = jax.tree.map(
        lambda part, zero: jnp.full_like(part, 0) + jnp.asarray(zero, part.dtype), value, neutral
    )

    def lap(position, so_far):
        longer = join(so_far, jax.tree.map(lambda part: part[position], pieces))
        return jax.tree.map(lambda new, old: jnp.where(position < mine, new, old), longer, so_far)

    return lax.fori_loop(0, count - 1, lap, so_far)


def gelu_tanh(values):
    return jax.nn.gelu(values, approximate=True)


def gelu_slope(values):
    _, pullback = jax.vjp(gelu_tanh, values)
    return pullback(jnp.ones_like(values))[0]


def bdot(left, right):
    return jnp.dot(left, right, preferred_element_type=jnp.float32)


def link_pairs(earlier, later):
    return (earlier[0] * later[0], later[0] * earlier[1] + later[1])


def per_device(
    block_input,
    mix_gain,
    x_weight,
    y_weight,
    conv_weight,
    conv_bias,
    input_gate,
    decay_gate,
    decay_param,
    out_weight,
    ffn_gain,
    gate_weight,
    up_weight,
    down_weight,
    out_cotangent,
):
    seq_count, group_len, model_width = block_input.shape
    local_w = x_weight.shape[1]
    head_size = input_gate.shape[0]
    full_w = local_w * lax.axis_size("mp")
    row_count = seq_count * group_len
    owner = lax.axis_index("mp")
    row_heads = jnp.arange(full_w, dtype=jnp.int32) // head_size
    col_heads = (owner * local_w + jnp.arange(local_w, dtype=jnp.int32)) // head_size
    head_mask = row_heads[:, None] == col_heads[None, :]
    dense_x = jnp.where(
        head_mask, jnp.tile(input_gate, (full_w // head_size, 1)), jnp.zeros((), jnp.bfloat16)
    )
    dense_a = jnp.where(
        head_mask, jnp.tile(decay_gate, (full_w // head_size, 1)), jnp.zeros((), jnp.bfloat16)
    )
    inp = block_input.reshape(row_count, model_width).astype(jnp.float32)
    r_one = lax.rsqrt(jnp.mean(inp * inp, axis=-1, keepdims=True) + EPS)
    n_one = inp * r_one
    normed1 = (n_one * mix_gain).astype(jnp.bfloat16)
    x_branch = bdot(normed1, x_weight)
    y_branch = bdot(normed1, y_weight)
    y_gated = gelu_tanh(y_branch)
    x_three = x_branch.reshape(seq_count, group_len, local_w)
    before = passed_along(x_three[:, group_len - 3 :, :], "seq", 1)
    padded = jnp.concatenate([before, x_three], axis=1)
    conv_three = conv_bias + sum(
        (conv_weight[offset] * padded[:, offset : offset + group_len] for offset in range(4))
    )
    conv_out = conv_three.reshape(row_count, local_w)
    conv_low = conv_out.astype(jnp.bfloat16)
    gathered = lax.all_gather(conv_low, "mp", axis=1, tiled=True)
    gate_x = jax.nn.sigmoid(bdot(gathered, dense_x))
    gate_a = jax.nn.sigmoid(bdot(gathered, dense_a))
    softer = jax.nn.softplus(decay_param)
    log_decay = -8.0 * softer * gate_a
    decay = jnp.exp(log_decay)
    mult = jnp.sqrt(-jnp.expm1(2.0 * log_decay))
    drive = conv_out * gate_x * mult
    decay_three = decay.reshape(seq_count, group_len, local_w)
    prod_three, local_state = lax.associative_scan(
        link_pairs, (decay_three, drive.reshape(seq_count, group_len, local_w)), axis=1
    )
    block_prod = prod_three[:, -1]
    ones_init = jnp.ones((seq_count, local_w), jnp.float32)
    zero_init = jnp.zeros((seq_count, local_w), jnp.float32)
    carried = carried_in(
        (block_prod, local_state[:, -1]), "seq", link_pairs, (ones_init, zero_init), False
    )
    state_in = carried[1]
    hidden_three = local_state + prod_three * state_in[:, None, :]
    hidden = hidden_three.reshape(row_count, local_w)
    mixed = (hidden * y_gated).astype(jnp.bfloat16)
    x_one = inp + lax.psum(bdot(mixed, out_weight), "mp")
    r_two = lax.rsqrt(jnp.mean(x_one * x_one, axis=-1, keepdims=True) + EPS)
    n_two = x_one * r_two
    normed2 = (n_two * ffn_gain).astype(jnp.bfloat16)
    gate_pre = bdot(normed2, gate_weight)
    up_pre = bdot(normed2, up_weight)
    act = (gelu_tanh(gate_pre) * up_pre).astype(jnp.bfloat16)
    ffn_out = lax.psum(bdot(act, down_weight), "mp")
    block_output = (x_one + ffn_out).astype(jnp.bfloat16).reshape(seq_count, group_len, model_width)
    cot_low = out_cotangent.reshape(row_count, model_width)
    cot = cot_low.astype(jnp.float32)
    d_act = bdot(cot_low, down_weight.T)
    g_down = bdot(act.T, cot_low)
    d_gate = (d_act * up_pre * gelu_slope(gate_pre)).astype(jnp.bfloat16)
    d_up = (d_act * gelu_tanh(gate_pre)).astype(jnp.bfloat16)
    g_gate = bdot(normed2.T, d_gate)
    g_up = bdot(normed2.T, d_up)
    d_n_two = lax.psum(bdot(d_gate, gate_weight.T) + bdot(d_up, up_weight.T), "mp")
    g_ffn_gain = jnp.sum(d_n_two * n_two, axis=0)
    e_two = ffn_gain * d_n_two
    d_x_one = cot + r_two * (e_two - n_two * jnp.mean(e_two * n_two, axis=-1, keepdims=True))
    d_x_low = d_x_one.astype(jnp.bfloat16)
    g_out = bdot(mixed.T, d_x_low)
    d_mixed = bdot(d_x_low, out_weight.T)
    d_y_low = (d_mixed * hidden * gelu_slope(y_branch)).astype(jnp.bfloat16)
    direct = (d_mixed * y_gated).reshape(seq_count, group_len, local_w)
    decay_next = jnp.concatenate(
        [decay_three[:, 1:], jnp.ones((seq_count, 1, local_w), jnp.float32)], axis=1
    )
    after_prod, local_lam = lax.associative_scan(
        link_pairs, (decay_next, direct), reverse=True, axis=1
    )
    first_term = decay_three[:, 0] * local_lam[:, 0]
    returned = carried_in((block_prod, first_term), "seq", link_pairs, (ones_init, zero_init), True)
    lam = (local_lam + after_prod * returned[1][:, None, :]).reshape(row_count, local_w)
    hidden_prev = jnp.concatenate([state_in[:, None, :], hidden_three[:, :-1]], axis=1).reshape(
        row_count, local_w
    )
    d_log = lam * hidden_prev * decay - lam * conv_out * gate_x * decay * decay / mult
    g_decay = jnp.sum(d_log * (-8.0 * gate_a) * jax.nn.sigmoid(decay_param), axis=0)
    d_gx = (lam * conv_out * mult * gate_x * (1.0 - gate_x)).astype(jnp.bfloat16)
    d_ga = (d_log * (-8.0 * softer) * gate_a * (1.0 - gate_a)).astype(jnp.bfloat16)
    dense_gx = jnp.where(head_mask, bdot(gathered.T, d_gx), 0.0)
    dense_ga = jnp.where(head_mask, bdot(gathered.T, d_ga), 0.0)
    g_input_gate = jnp.sum(dense_gx.reshape(full_w // head_size, head_size, local_w), axis=0)
    g_decay_gate = jnp.sum(dense_ga.reshape(full_w // head_size, head_size, local_w), axis=0)
    back_terms = bdot(d_gx, dense_x.T) + bdot(d_ga, dense_a.T)
    back_own = lax.psum_scatter(back_terms, "mp", scatter_dimension=1, tiled=True)
    d_conv = lam * gate_x * mult + back_own
    g_conv_bias = jnp.sum(d_conv, axis=0)
    d_conv_three = d_conv.reshape(seq_count, group_len, local_w)
    g_conv = jnp.stack(
        [
            jnp.sum(d_conv_three * padded[:, offset : offset + group_len], axis=(0, 1))
            for offset in range(4)
        ]
    )
    later_rows = passed_along(d_conv_three[:, :3, :], "seq", -1)
    padded_back = jnp.concatenate([d_conv_three, later_rows], axis=1)
    d_x_three = sum(
        (
            conv_weight[offset] * padded_back[:, 3 - offset : 3 - offset + group_len]
            for offset in range(4)
        )
    )
    d_x_branch = d_x_three.reshape(row_count, local_w).astype(jnp.bfloat16)
    g_x = bdot(normed1.T, d_x_branch)
    g_y = bdot(normed1.T, d_y_low)
    d_n_one = lax.psum(bdot(d_x_branch, x_weight.T) + bdot(d_y_low, y_weight.T), "mp")
    g_mix_gain = jnp.sum(d_n_one * n_one, axis=0)
    e_one = mix_gain * d_n_one
    d_input = d_x_one + r_one * (e_one - n_one * jnp.mean(e_one * n_one, axis=-1, keepdims=True))
    input_grad = d_input.astype(jnp.bfloat16).reshape(seq_count, group_len, model_width)
    summed = (
        lax.psum_scatter(g_mix_gain, "seq", scatter_dimension=0, tiled=True),
        lax.psum_scatter(g_x, "seq", scatter_dimension=0, tiled=True),
        lax.psum_scatter(g_y, "seq", scatter_dimension=0, tiled=True),
        lax.psum_scatter(g_conv, "seq", scatter_dimension=1, tiled=True),
        lax.psum_scatter(g_conv_bias, "seq", scatter_dimension=0, tiled=True),
        lax.psum_scatter(g_input_gate, "seq", scatter_dimension=0, tiled=True),
        lax.psum_scatter(g_decay_gate, "seq", scatter_dimension=0, tiled=True),
        lax.psum_scatter(g_decay, "seq", scatter_dimension=0, tiled=True),
        lax.psum_scatter(g_out, "seq", scatter_dimension=1, tiled=True),
        lax.psum_scatter(g_ffn_gain, "seq", scatter_dimension=0, tiled=True),
        lax.psum_scatter(g_gate, "seq", scatter_dimension=0, tiled=True),
        lax.psum_scatter(g_up, "seq", scatter_dimension=0, tiled=True),
        lax.psum_scatter(g_down, "seq", scatter_dimension=1, tiled=True),
    )
    return (
        block_output,
        input_grad,
        summed[0],
        summed[1],
        summed[2],
        summed[3],
        summed[4],
        summed[5],
        summed[6],
        summed[7],
        summed[8],
        summed[9],
        summed[10],
        summed[11],
        summed[12],
    )


def solution(mesh):
    in_specs = (
        P(None, "seq", None),
        P(),
        P(None, "mp"),
        P(None, "mp"),
        P(None, "mp"),
        P("mp"),
        P(None, "mp"),
        P(None, "mp"),
        P("mp"),
        P("mp", None),
        P(),
        P(None, "mp"),
        P(None, "mp"),
        P("mp", None),
        P(None, "seq", None),
    )
    out_specs = (
        P(None, "seq", None),
        P(None, "seq", None),
        P("seq"),
        P("seq", "mp"),
        P("seq", "mp"),
        P(None, ("mp", "seq")),
        P(("mp", "seq")),
        P("seq", "mp"),
        P("seq", "mp"),
        P(("mp", "seq")),
        P("mp", "seq"),
        P("seq"),
        P("seq", "mp"),
        P("seq", "mp"),
        P("mp", "seq"),
    )
    return jax.shard_map(
        per_device, mesh=mesh, in_specs=in_specs, out_specs=out_specs, check_vma=False
    )
```

profile of v0, /device:TPU:0, one launch (start us, length us, event | category | flops | bytes accessed | tf_op | source)
XLA Modules:
  0.0 2168.8 jit_solution(16874175498636065759)
XLA Ops:
  8.8 3.1 fusion.102
  12.6 4.9 collective-permute-start
  21.0 8.8 all_gather.14
  111.2 30.8 %all_gather.15 = f32[8,1,640]{2,1,0:T(1,128)S(1)} all-gather(f32[1,1,640]{2,1,0:T(1,128)S(1)} %slice_add_fusion.2), channel_id=1, replica_groups=mesh['seq'=8,'mp'=4] {'seq'}, dimensions={0}, use_global_device_ids=true | all-gather | bytes 23040 | tf_op jit(solution)/shard_map/all_gather | solution.py:17
  145.3 30.4 %all_gather.16 = f32[8,1,640]{2,1,0:T(1,128)S(1)} all-gather(f32[1,1,640]{2,1,0:T(1,128)S(1)} %slice_add_fusion.1), channel_id=1, replica_groups=mesh['seq'=8,'mp'=4] {'seq'}, dimensions={0}, use_global_device_ids=true | all-gather | bytes 23040 | tf_op jit(solution)/shard_map/all_gather | solution.py:17
  176.1 3.6 fusion.67
  182.2 42.2 %all-reduce.68.cloned.1.call-done = f32[160,2560]{1,0:T(8,128)} async-done(((f32[160,2560]{1,0:T(8,128)}), f32[160,2560]{1,0:T(8,128)}) %all-reduce.68.cloned.1.call-update) | async-done | bytes 1638416 | tf_op jit(solution)/shard_map/psum | solution.py:118
  227.8 6.2 fusion.118
  236.5 8.1 multiply_convert_fusion.1
  244.5 3.3 fusion.120
  247.9 8.3 convolution_add_fusion.2
  264.0 3.0 slice.534
  267.0 3.0 slice.527
  270.1 3.0 slice.529
  273.1 27.3 %all-reduce.70.cloned.1.call-done = f32[160,2560]{1,0:T(8,128)} async-done(((f32[160,2560]{1,0:T(8,128)}), f32[160,2560]{1,0:T(8,128)}) %all-reduce.70.cloned.1.call-update) | async-done | bytes 1638416 | tf_op jit(solution)/shard_map/psum | solution.py:135
  300.4 3.2 multiply_reduce_fusion
  308.1 5.6 reverse.8
  433.8 2.5 pad.215
  440.6 5.6 rev.17
  446.2 30.5 %all_gather.17 = f32[8,1,640]{2,1,0:T(1,128)S(1)} all-gather(f32[1,1,640]{2,1,0:T(1,128)S(1)} %add_multiply_fusion.20), channel_id=1, replica_groups=mesh['seq'=8,'mp'=4] {'seq'}, dimensions={0}, use_global_device_ids=true | all-gather | bytes 23040 | tf_op jit(solution)/shard_map/all_gather | solution.py:17
  476.7 4.8 while.29
  484.0 2.5 pad.229
  488.4 5.6 rev.18
  502.8 7.1 fusion.119
  509.8 21.3 reduce-scatter.13.cloned.1.call-done
  537.1 3.5 collective-permute-done.1
  542.5 3.3 fusion.78
  549.5 3.6 compare_select_fusion
  553.0 4.2 reduce_sum.137
  557.3 3.6 compare_select_fusion.1
  560.9 4.2 reduce_sum.136
  565.2 4.0 fusion.71
  570.3 4.0 fusion.98
  575.3 4.1 fusion.33
  580.7 8.4 fusion.36
  590.4 8.2 fusion.123
  599.7 8.4 fusion.122
  612.1 60.4 %all-reduce.72.cloned.1.call-done = (f32[160,2560]{1,0:T(8,128)}, f32[160,2560]{1,0:T(8,128)}) async-done(((f32[160,2560]{1,0:T(8,128)}, f32[160,2560]{1,0:T(8,128)}), (f32[160,2560]{1,0:T(8,128)}, f32[160,2560]{1,0:T(8,128)})) %all-reduce.72.cloned.1.call-update) | async-done | bytes 3276816 | tf_op jit(solution)/shard_map/psum | solution.py:125
  674.5 37.3 %all-reduce.62 = (f32[2560]{0:T(1024)S(1)}, f32[640]{0:T(1024)S(1)}, f32[640]{0:T(1024)S(1)}, f32[2560]{0:T(1024)S(1)}) all-reduce(f32[2560]{0:T(1024)S(1)} %get-tuple-element.243, f32[640]{0:T(1024)S(1)} %get-tuple-element.248, f32[640]{0:T(1024)S(1)} %get-tuple-element.281, ...), channel_id=3, replica_groups=mesh['seq'=8,'mp'=4] {'seq'}, use_global_device_ids=true, to_apply=%region_14.15.clone | all-reduce | flops 6400 | bytes 51200
  714.3 3.1 fusion.31
  718.9 20.2 reduce-scatter.21.cloned.1.call-done
  739.1 65.6 %reduce-scatter.19.cloned.1.call-done = f32[32,640]{1,0:T(8,128)} async-done(((f32[256,640]{1,0:T(8,128)}), f32[32,640]{1,0:T(8,128)}) %reduce-scatter.19.cloned.1.call-update) | async-done | bytes 81936 | tf_op jit(solution)/shard_map/reduce_scatter | solution.py:197
  804.7 125.0 %reduce-scatter.23.cloned.1.call-done = f32[640,320]{0,1:T(8,128)} async-done(((f32[640,2560]{0,1:T(8,128)}), f32[640,320]{0,1:T(8,128)}) %reduce-scatter.23.cloned.1.call-update) | async-done | bytes 819216 | tf_op jit(solution)/shard_map/reduce_scatter | solution.py:200
  929.8 125.2 %reduce-scatter.17.cloned.1.call-done = f32[320,640]{1,0:T(8,128)} async-done(((f32[2560,640]{1,0:T(8,128)}), f32[320,640]{1,0:T(8,128)}) %reduce-scatter.17.cloned.1.call-update) | async-done | bytes 819216 | tf_op jit(solution)/shard_map/reduce_scatter | solution.py:194
  1055.0 125.1 %reduce-scatter.15.cloned.1.call-done = f32[320,640]{1,0:T(8,128)} async-done(((f32[2560,640]{1,0:T(8,128)}), f32[320,640]{1,0:T(8,128)}) %reduce-scatter.15.cloned.1.call-update) | async-done | bytes 819216 | tf_op jit(solution)/shard_map/reduce_scatter | solution.py:193
  1180.1 327.6 %reduce-scatter.29.cloned.1.call-done = f32[1920,320]{0,1:T(8,128)} async-done(((f32[1920,2560]{0,1:T(8,128)}), f32[1920,320]{0,1:T(8,128)}) %reduce-scatter.29.cloned.1.call-update) | async-done | bytes 2457616 | tf_op jit(solution)/shard_map/reduce_scatter | solution.py:204
  1507.6 327.2 %reduce-scatter.27.cloned.1.call-done = f32[320,1920]{1,0:T(8,128)} async-done(((f32[2560,1920]{1,0:T(8,128)}), f32[320,1920]{1,0:T(8,128)}) %reduce-scatter.27.cloned.1.call-update) | async-done | bytes 2457616 | tf_op jit(solution)/shard_map/reduce_scatter | solution.py:203
  1834.8 327.2 %reduce-scatter.25.cloned.1.call-done = f32[320,1920]{1,0:T(8,128)} async-done(((f32[2560,1920]{1,0:T(8,128)}), f32[320,1920]{1,0:T(8,128)}) %reduce-scatter.25.cloned.1.call-update) | async-done | bytes 2457616 | tf_op jit(solution)/shard_map/reduce_scatter | solution.py:202
  (486 shorter events, 279.0 us)
Async XLA Ops:
  7.2 168.8 %copy-start = (bf16[2560,640]{1,0:T(8,128)(2,1)S(1)}, bf16[2560,640]{1,0:T(8,128)(2,1)}, u32[]{:S(2)}) copy-start(bf16[2560,640]{1,0:T(8,128)(2,1)} %param.22) | copy-start | bytes 9830404
  7.2 217.2 %all-reduce.68.cloned.1.call-start = ((), (), s32[]{:S(2)}) async-start(), calls=%async_computation.10 | async-start | bytes 3276800 | tf_op jit(solution)/shard_map/psum | solution.py:118
  8.8 167.2 %copy-start.59 = (f32[160]{0:T(256)}, f32[160]{0:T(256)S(1)}, u32[]{:S(2)}) copy-start(f32[160]{0:T(256)S(1)} %add_rsqrt_fusion.1) | copy-start | bytes 1924
  8.8 8.8 copy-start.82
  8.8 9.4 copy-start.79
  12.6 8.1 collective-permute-start
  18.2 13.4 copy-start.56
  20.7 9.9 copy-start.13
  20.7 9.9 copy-start.11
  20.8 9.9 copy-start.64
  21.0 10.5 copy-start.21
  100.1 8.8 copy-start.77
  106.9 69.2 %copy-start.50 = (f32[2560]{0:T(1024)S(1)}, f32[2560]{0:T(1024)}, u32[]{:S(2)}) copy-start(f32[2560]{0:T(1024)} %param.20) | copy-start | bytes 30724
  176.0 3.6 copy-start.53
  181.7 45.9 %copy-start.55 = (f32[2560]{0:T(1024)S(1)}, f32[2560]{0:T(1024)}, u32[]{:S(2)}) copy-start(f32[2560]{0:T(1024)} %param.29) | copy-start | bytes 30724
  181.7 118.7 %all-reduce.70.cloned.1.call-start = ((), (), s32[]{:S(2)}) async-start(), calls=%async_computation.11 | async-start | bytes 3276800 | tf_op jit(solution)/shard_map/psum | solution.py:135
  227.6 6.4 slice-start
  227.8 6.2 copy-start.6
  227.8 6.3 slice-start.1
  227.8 6.7 slice-start.2
  256.2 274.9 %reduce-scatter.13.cloned.1.call-start = ((), (), s32[]{:S(2)}) async-start(), calls=%async_computation.12 | async-start | bytes 2048000 | tf_op jit(solution)/shard_map/reduce_scatter | solution.py:165
  407.9 8.6 copy-start.80
  422.7 7.9 copy-start.78
  433.8 42.9 %copy-start.58 = (f32[1,640]{1,0:T(1,128)S(1)}, f32[1,640]{1,0:T(1,128)}, u32[]{:S(2)}) copy-start(f32[1,640]{1,0:T(1,128)} %custom-call.1) | copy-start | bytes 7684
  481.5 12.6 copy-start.54
  481.5 12.6 copy-start.57
  481.5 12.6 copy-start.76
  494.1 4.1 copy-start.14
  502.7 108.0 %reduce-scatter.31.cloned.1.call-start = ((), (), s32[]{:S(2)}) async-start(), calls=%async_computation.21 | async-start | bytes 368640
  502.8 28.4 %copy-start.65 = (f32[1,3,640]{2,1,0:T(4,128)S(1)}, f32[1,3,640]{2,1,0:T(4,128)}, u32[]{:S(2)}) copy-start(f32[1,3,640]{2,1,0:T(4,128)} %copy-done.64) | copy-start | bytes 23044
  509.8 30.8 %copy-start.67 = (f32[640]{0:T(1024)S(1)}, f32[640]{0:T(1024)}, u32[]{:S(2)}) copy-start(f32[640]{0:T(1024)} %copy-done.66) | copy-start | bytes 7684
  509.8 30.8 %copy-start.69 = (f32[640]{0:T(1024)S(1)}, f32[640]{0:T(1024)}, u32[]{:S(2)}) copy-start(f32[640]{0:T(1024)} %copy-done.68) | copy-start | bytes 7684
  509.8 30.8 %copy-start.71 = (f32[640]{0:T(1024)S(1)}, f32[640]{0:T(1024)}, u32[]{:S(2)}) copy-start(f32[640]{0:T(1024)} %copy-done.70) | copy-start | bytes 7684
  509.8 30.8 %copy-start.73 = (f32[640]{0:T(1024)S(1)}, f32[640]{0:T(1024)}, u32[]{:S(2)}) copy-start(f32[640]{0:T(1024)} %copy-done.72) | copy-start | bytes 7684
  534.8 5.8 collective-permute-start.1
  537.1 135.4 %all-reduce.72.cloned.1.call-start = ((), (), s32[]{:S(2)}) async-start(), calls=%async_computation.22 | async-start | bytes 6553600 | tf_op jit(solution)/shard_map/psum | solution.py:125
  548.3 190.8 %reduce-scatter.21.cloned.1.call-start = ((), (), s32[]{:S(2)}) async-start(), calls=%async_computation.16 | async-start | bytes 737280 | tf_op jit(solution)/shard_map/reduce_scatter | solution.py:198
  553.0 4.2 copy-start.46
  557.2 247.5 %reduce-scatter.19.cloned.1.call-start = ((), (), s32[]{:S(2)}) async-start(), calls=%async_computation.15 | async-start | bytes 737280 | tf_op jit(solution)/shard_map/reduce_scatter | solution.py:197
  560.9 4.3 copy-start.9
  565.1 364.7 %reduce-scatter.23.cloned.1.call-start = ((), (), s32[]{:S(2)}) async-start(), calls=%async_computation.17 | async-start | bytes 7372800 | tf_op jit(solution)/shard_map/reduce_scatter | solution.py:200
  569.2 485.8 %reduce-scatter.17.cloned.1.call-start = ((), (), s32[]{:S(2)}) async-start(), calls=%async_computation.14 | async-start | bytes 7372800 | tf_op jit(solution)/shard_map/reduce_scatter | solution.py:194
  574.4 605.7 %reduce-scatter.15.cloned.1.call-start = ((), (), s32[]{:S(2)}) async-start(), calls=%async_computation.13 | async-start | bytes 7372800 | tf_op jit(solution)/shard_map/reduce_scatter | solution.py:193
  579.4 928.2 %reduce-scatter.29.cloned.1.call-start = ((), (), s32[]{:S(2)}) async-start(), calls=%async_computation.20 | async-start | bytes 22118400 | tf_op jit(solution)/shard_map/reduce_scatter | solution.py:204
  589.1 1245.7 %reduce-scatter.27.cloned.1.call-start = ((), (), s32[]{:S(2)}) async-start(), calls=%async_computation.19 | async-start | bytes 22118400 | tf_op jit(solution)/shard_map/reduce_scatter | solution.py:203
  598.6 1563.4 %reduce-scatter.25.cloned.1.call-start = ((), (), s32[]{:S(2)}) async-start(), calls=%async_computation.18 | async-start | bytes 22118400 | tf_op jit(solution)/shard_map/reduce_scatter | solution.py:202
  608.1 66.3 %copy-start.63 = (f32[2560]{0:T(1024)S(1)}, f32[2560]{0:T(1024)}, u32[]{:S(2)}) copy-start(f32[2560]{0:T(1024)} %get-tuple-element.241) | copy-start | bytes 30724
  714.3 1447.8 %copy-start.1 = (bf16[2560,640]{1,0:T(8,128)(2,1)S(1)}, bf16[2560,640]{1,0:T(8,128)(2,1)}, u32[]{:S(2)}) copy-start(bf16[2560,640]{1,0:T(8,128)(2,1)} %param.22) | copy-start | bytes 9830404
  (54 other events, 99.0 us)
Sparse Core Ops, SparseCore 0:
  181.8 42.5 all-reduce.67
  256.4 43.9 all-reduce.69
  502.8 28.2 reduce-scatter.12
  537.2 63.3 reduce-scatter.30
  602.8 69.6 all-reduce.71
  676.2 62.8 reduce-scatter.20
  743.0 61.7 reduce-scatter.18
  808.9 120.8 reduce-scatter.22
  934.0 120.9 reduce-scatter.16
  1059.0 120.9 reduce-scatter.14
  1184.6 323.0 reduce-scatter.28
  1512.0 322.7 reduce-scatter.26
  1839.3 322.7 reduce-scatter.24
where the time goes:
time: 2180 us; the launch traced here: 2170 us
  waiting for transfers between devices  1600 us (73%)
  local copies, waits for them, and re-layouts  193 us (9%)
  blocking collectives  138 us (6%)
  other arithmetic  115 us (5%)
  matrix products  101 us (5%)
    reduce_scatter x1, waiting for transfers between devices, per_device(): lax.psum_scatter(g_down, 'seq', scatter_dimension=1, tiled=True)  328 us
    reduce_scatter x1, waiting for transfers between devices, per_device(): lax.psum_scatter(g_gate, 'seq', scatter_dimension=0, tiled=True)  327 us
    reduce_scatter x1, waiting for transfers between devices, per_device(): lax.psum_scatter(g_up, 'seq', scatter_dimension=0, tiled=True)  327 us
    reduce_scatter x1, waiting for transfers between devices, per_device(): lax.psum_scatter(g_y, 'seq', scatter_dimension=0, tiled=True)  125 us
    reduce_scatter x1, waiting for transfers between devices, per_device(): lax.psum_scatter(g_x, 'seq', scatter_dimension=0, tiled=True)  125 us
    reduce_scatter x1, waiting for transfers between devices, per_device(): lax.psum_scatter(g_out, 'seq', scatter_dimension=1, tiled=True)  125 us
    dot_general x24, matrix products, bdot(): return jnp.dot(left, right, preferred_element_type=jnp.float32)  101 us
    all_gather x3, blocking collectives, carried_in(): pieces = jax.tree.map(lambda part: lax.all_gather(part, axis), value)  91.7 us
  transfers between devices with their start and end apart: 15, of which 13 were waited for; matrix products, arithmetic and copies ran while one was open for 5% of the time, Pallas kernels for 0%

commit v1 on v0

--- a/solution.py
+++ b/solution.py
@@ -4,6 +4,7 @@
 from jax.sharding import PartitionSpec as P
 
 EPS = 1e-06
+run_proceed = lambda field_in: lax.all_gather(field_in, "mp").sum(axis=0)
 
 
 def passed_along(shard, axis, by):
@@ -122,7 +123,7 @@
     gate_pre = bdot(normed2, gate_weight)
     up_pre = bdot(normed2, up_weight)
     act = (gelu_tanh(gate_pre) * up_pre).astype(jnp.bfloat16)
-    ffn_out = lax.psum(bdot(act, down_weight), "mp")
+    ffn_out = run_proceed(bdot(act, down_weight))
     block_output = (x_one + ffn_out).astype(jnp.bfloat16).reshape(seq_count, group_len, model_width)
     cot_low = out_cotangent.reshape(row_count, model_width)
     cot = cot_low.astype(jnp.float32)

time: 2180 us -> 2270 us (1.041)
  local copies, waits for them, and re-layouts: 193 us -> 240 us
    all_gather x0 -> x1, waiting for transfers between devices: none -> 47 us  [run_proceed = lambda field_in: lax.all_gather(field_in, 'mp').sum(axis=0)]
    reduce_scatter x1, waiting for transfers between devices: 20.2 us -> 65.6 us  [per_device(): lax.psum_scatter(g_decay_gate, 'seq', scatter_dimension=0, tiled=True)]
    reduce_scatter x1, waiting for transfers between devices: 65.6 us -> 21.1 us  [per_device(): lax.psum_scatter(g_input_gate, 'seq', scatter_dimension=0, tiled=True)]
    slice x48, local copies, waits for them, and re-layouts: 27.7 us -> 62.4 us  [per_device(): lax.associative_scan(link_pairs, (decay_three, drive.reshape(seq_count, g...]
    psum x1, waiting for transfers between devices: 60.4 us -> 33.6 us  [per_device(): lax.psum(bdot(d_x_branch, x_weight.T) + bdot(d_y_low, y_weight.T), 'mp')]
  transfers between devices with their start and end apart: 15 -> 16, of which waited for: 13 -> 14; matrix products, arithmetic and copies ran while one was open for 5% -> 4% of each run, Pallas kernels for 0% -> 0%
where the time goes in v1:
time: 2270 us; the launch traced here: 2250 us
  waiting for transfers between devices  1620 us (71%)
  local copies, waits for them, and re-layouts  240 us (11%)
  blocking collectives  138 us (6%)
  other arithmetic  132 us (6%)
  matrix products  101 us (4%)
    reduce_scatter x1, waiting for transfers between devices, per_device(): lax.psum_scatter(g_gate, 'seq', scatter_dimension=0, tiled=True)  327 us
    reduce_scatter x1, waiting for transfers between devices, per_device(): lax.psum_scatter(g_up, 'seq', scatter_dimension=0, tiled=True)  327 us
    reduce_scatter x1, waiting for transfers between devices, per_device(): lax.psum_scatter(g_down, 'seq', scatter_dimension=1, tiled=True)  327 us
    reduce_scatter x1, waiting for transfers between devices, per_device(): lax.psum_scatter(g_x, 'seq', scatter_dimension=0, tiled=True)  125 us
    reduce_scatter x1, waiting for transfers between devices, per_device(): lax.psum_scatter(g_y, 'seq', scatter_dimension=0, tiled=True)  125 us
    reduce_scatter x1, waiting for transfers between devices, per_device(): lax.psum_scatter(g_out, 'seq', scatter_dimension=1, tiled=True)  125 us
    dot_general x24, matrix products, bdot(): return jnp.dot(left, right, preferred_element_type=jnp.float32)  101 us
    all_gather x3, blocking collectives, carried_in(): pieces = jax.tree.map(lambda part: lax.all_gather(part, axis), value)  91.7 us
  transfers between devices with their start and end apart: 16, of which 14 were waited for; matrix products, arithmetic and copies ran while one was open for 4% of the time, Pallas kernels for 0%

profile of v1, /device:TPU:0, one launch (start us, length us, event | category | flops | bytes accessed | tf_op | source)
XLA Modules:
  0.0 2254.9 jit_solution(7385648948670464965)
XLA Ops:
  8.8 3.1 fusion.102
  12.6 4.9 collective-permute-start
  21.1 8.8 all_gather.20
  150.5 30.8 %all_gather.22 = f32[8,1,640]{2,1,0:T(1,128)S(1)} all-gather(f32[1,1,640]{2,1,0:T(1,128)S(1)} %slice_add_fusion.1), channel_id=1, replica_groups=mesh['seq'=8,'mp'=4] {'seq'}, dimensions={0}, use_global_device_ids=true | all-gather | bytes 23040 | tf_op jit(solution)/shard_map/all_gather | solution.py:18
  187.7 30.4 %all_gather.21 = f32[8,1,640]{2,1,0:T(1,128)S(1)} all-gather(f32[1,1,640]{2,1,0:T(1,128)S(1)} %slice_add_fusion.2), channel_id=1, replica_groups=mesh['seq'=8,'mp'=4] {'seq'}, dimensions={0}, use_global_device_ids=true | all-gather | bytes 23040 | tf_op jit(solution)/shard_map/all_gather | solution.py:18
  218.5 3.5 fusion.67
  224.6 42.2 %all-reduce.67.cloned.1.call-done = f32[160,2560]{1,0:T(8,128)} async-done(((f32[160,2560]{1,0:T(8,128)}), f32[160,2560]{1,0:T(8,128)}) %all-reduce.67.cloned.1.call-update) | async-done | bytes 1638416 | tf_op jit(solution)/shard_map/psum | solution.py:119
  270.1 6.2 fusion.117
  278.7 8.8 multiply_convert_fusion.1
  287.6 3.3 fusion.120
  290.9 8.3 convolution_add_fusion.2
  299.3 7.0 fusion.119
  314.1 3.0 slice.529
  320.2 3.0 slice.527
  323.2 20.2 all-reduce.69.cloned.1.call-done
  343.4 3.0 multiply_reduce_fusion
  346.5 47.0 %all-gather.3.cloned.1.call-done = f32[640,2560]{1,0:T(8,128)} async-done(((f32[160,2560]{1,0:T(8,128)}), f32[640,2560]{1,0:T(8,128)}) %all-gather.3.cloned.1.call-update) | async-done | bytes 6553616 | tf_op jit(solution)/shard_map/all_gather | solution.py:7
  393.5 4.7 reduce_sum.137
  398.2 4.4 multiply_add_fusion
  404.7 5.6 reverse.8
  551.5 30.5 %all_gather.25 = f32[8,1,640]{2,1,0:T(1,128)S(1)} all-gather(f32[1,1,640]{2,1,0:T(1,128)S(1)} %add_multiply_fusion.20), channel_id=1, replica_groups=mesh['seq'=8,'mp'=4] {'seq'}, dimensions={0}, use_global_device_ids=true | all-gather | bytes 23040 | tf_op jit(solution)/shard_map/all_gather | solution.py:18
  582.0 4.8 while.29
  595.4 5.6 rev.18
  601.0 5.6 rev.17
  615.3 28.3 %reduce-scatter.13.cloned.1.call-done = f32[160,640]{1,0:T(8,128)} async-done(((f32[160,2560]{1,0:T(8,128)}), f32[160,640]{1,0:T(8,128)}) %reduce-scatter.13.cloned.1.call-update) | async-done | bytes 409616 | tf_op jit(solution)/shard_map/reduce_scatter | solution.py:166
  649.7 3.5 collective-permute-done.1
  655.1 3.3 fusion.78
  662.0 3.6 compare_select_fusion.1
  665.6 4.2 reduce_sum.146
  669.8 3.6 compare_select_fusion
  673.4 4.2 reduce_sum.147
  677.7 4.0 fusion.71
  682.9 4.0 fusion.98
  687.9 4.1 fusion.33
  693.3 8.2 fusion.122
  702.5 8.2 fusion.123
  712.1 8.6 fusion.36
  724.7 33.6 %all-reduce.71.cloned.1.call-done = f32[160,2560]{1,0:T(8,128)} async-done(((f32[160,2560]{1,0:T(8,128)}), f32[160,2560]{1,0:T(8,128)}) %all-reduce.71.cloned.1.call-update) | async-done | bytes 1638416 | tf_op jit(solution)/shard_map/psum | solution.py:187
  760.3 37.4 %all-reduce.62 = (f32[2560]{0:T(1024)S(1)}, f32[640]{0:T(1024)S(1)}, f32[640]{0:T(1024)S(1)}, f32[2560]{0:T(1024)S(1)}) all-reduce(f32[2560]{0:T(1024)S(1)} %get-tuple-element.243, f32[640]{0:T(1024)S(1)} %get-tuple-element.248, f32[640]{0:T(1024)S(1)} %get-tuple-element.279, ...), channel_id=4, replica_groups=mesh['seq'=8,'mp'=4] {'seq'}, use_global_device_ids=true, to_apply=%region_14.15.clone | all-reduce | flops 6400 | bytes 51200
  800.3 3.7 fusion.35
  804.0 21.1 reduce-scatter.19.cloned.1.call-done
  825.1 65.6 %reduce-scatter.21.cloned.1.call-done = f32[32,640]{1,0:T(8,128)} async-done(((f32[256,640]{1,0:T(8,128)}), f32[32,640]{1,0:T(8,128)}) %reduce-scatter.21.cloned.1.call-update) | async-done | bytes 81936 | tf_op jit(solution)/shard_map/reduce_scatter | solution.py:199
  890.7 125.0 %reduce-scatter.23.cloned.1.call-done = f32[640,320]{0,1:T(8,128)} async-done(((f32[640,2560]{0,1:T(8,128)}), f32[640,320]{0,1:T(8,128)}) %reduce-scatter.23.cloned.1.call-update) | async-done | bytes 819216 | tf_op jit(solution)/shard_map/reduce_scatter | solution.py:201
  1015.7 125.1 %reduce-scatter.17.cloned.1.call-done = f32[320,640]{1,0:T(8,128)} async-done(((f32[2560,640]{1,0:T(8,128)}), f32[320,640]{1,0:T(8,128)}) %reduce-scatter.17.cloned.1.call-update) | async-done | bytes 819216 | tf_op jit(solution)/shard_map/reduce_scatter | solution.py:195
  1140.8 125.2 %reduce-scatter.15.cloned.1.call-done = f32[320,640]{1,0:T(8,128)} async-done(((f32[2560,640]{1,0:T(8,128)}), f32[320,640]{1,0:T(8,128)}) %reduce-scatter.15.cloned.1.call-update) | async-done | bytes 819216 | tf_op jit(solution)/shard_map/reduce_scatter | solution.py:194
  1266.0 327.5 %reduce-scatter.25.cloned.1.call-done = f32[320,1920]{1,0:T(8,128)} async-done(((f32[2560,1920]{1,0:T(8,128)}), f32[320,1920]{1,0:T(8,128)}) %reduce-scatter.25.cloned.1.call-update) | async-done | bytes 2457616 | tf_op jit(solution)/shard_map/reduce_scatter | solution.py:203
  1593.4 327.4 %reduce-scatter.27.cloned.1.call-done = f32[320,1920]{1,0:T(8,128)} async-done(((f32[2560,1920]{1,0:T(8,128)}), f32[320,1920]{1,0:T(8,128)}) %reduce-scatter.27.cloned.1.call-update) | async-done | bytes 2457616 | tf_op jit(solution)/shard_map/reduce_scatter | solution.py:204
  1920.9 327.3 %reduce-scatter.29.cloned.1.call-done = f32[1920,320]{0,1:T(8,128)} async-done(((f32[1920,2560]{0,1:T(8,128)}), f32[1920,320]{0,1:T(8,128)}) %reduce-scatter.29.cloned.1.call-update) | async-done | bytes 2457616 | tf_op jit(solution)/shard_map/reduce_scatter | solution.py:205
  (482 shorter events, 341.5 us)
Async XLA Ops:
  7.2 211.3 %copy-start = (bf16[2560,640]{1,0:T(8,128)(2,1)S(1)}, bf16[2560,640]{1,0:T(8,128)(2,1)}, u32[]{:S(2)}) copy-start(bf16[2560,640]{1,0:T(8,128)(2,1)} %param.22) | copy-start | bytes 9830404
  7.2 259.6 %all-reduce.67.cloned.1.call-start = ((), (), s32[]{:S(2)}) async-start(), calls=%async_computation.10 | async-start | bytes 3276800 | tf_op jit(solution)/shard_map/psum | solution.py:119
  8.8 209.6 %copy-start.51 = (f32[160]{0:T(256)}, f32[160]{0:T(256)S(1)}, u32[]{:S(2)}) copy-start(f32[160]{0:T(256)S(1)} %add_rsqrt_fusion.1) | copy-start | bytes 1924
  8.8 8.8 copy-start.72
  8.8 8.8 copy-start.75
  12.6 8.1 collective-permute-start
  18.3 13.3 copy-start.48
  20.7 9.9 copy-start.8
  20.8 10.0 copy-start.10
  20.8 9.9 copy-start.57
  21.1 10.5 copy-start.18
  88.0 18.3 copy-start.56
  88.0 22.4 copy-start.43
  97.8 12.5 copy-start.44
  136.4 7.7 copy-start.70
  144.1 37.2 %copy-start.35 = (f32[1,79,640]{2,1,0:T(8,128)S(1)}, f32[1,79,640]{2,1,0:T(8,128)}, u32[]{:S(2)}) copy-start(f32[1,79,640]{2,1,0:T(8,128)} %get-tuple-element.304) | copy-start | bytes 606724
  144.8 73.7 %copy-start.42 = (f32[2560]{0:T(1024)S(1)}, f32[2560]{0:T(1024)}, u32[]{:S(2)}) copy-start(f32[2560]{0:T(1024)} %param.20) | copy-start | bytes 30724
  224.0 45.9 %copy-start.47 = (f32[2560]{0:T(1024)S(1)}, f32[2560]{0:T(1024)}, u32[]{:S(2)}) copy-start(f32[2560]{0:T(1024)} %param.29) | copy-start | bytes 30724
  224.0 119.4 %all-reduce.69.cloned.1.call-start = ((), (), s32[]{:S(2)}) async-start(), calls=%async_computation.11 | async-start | bytes 3276800 | tf_op jit(solution)/shard_map/psum | solution.py:136
  276.8 10.7 slice-start
  276.8 10.7 slice-start.1
  278.7 8.9 slice-start.2
  299.3 94.2 %all-gather.3.cloned.1.call-start = ((), (), s32[]{:S(2)}) async-start(), calls=%async_computation.22 | async-start | bytes 8192000 | tf_op jit(solution)/shard_map/all_gather | solution.py:7
  306.4 337.3 %reduce-scatter.13.cloned.1.call-start = ((), (), s32[]{:S(2)}) async-start(), calls=%async_computation.12 | async-start | bytes 2048000 | tf_op jit(solution)/shard_map/reduce_scatter | solution.py:166
  522.1 13.5 copy-start.73
  535.6 10.0 copy-start.71
  543.5 38.5 %copy-start.50 = (f32[1,640]{1,0:T(1,128)S(1)}, f32[1,640]{1,0:T(1,128)}, u32[]{:S(2)}) copy-start(f32[1,640]{1,0:T(1,128)} %custom-call.1) | copy-start | bytes 7684
  591.0 15.6 copy-start.46
  591.0 15.6 copy-start.49
  591.0 15.6 copy-start.69
  615.2 28.5 %copy-start.58 = (f32[1,3,640]{2,1,0:T(4,128)S(1)}, f32[1,3,640]{2,1,0:T(4,128)}, u32[]{:S(2)}) copy-start(f32[1,3,640]{2,1,0:T(4,128)} %copy-done.57) | copy-start | bytes 23044
  615.2 37.9 %copy-start.60 = (f32[640]{0:T(1024)S(1)}, f32[640]{0:T(1024)}, u32[]{:S(2)}) copy-start(f32[640]{0:T(1024)} %copy-done.59) | copy-start | bytes 7684
  615.2 37.9 %copy-start.62 = (f32[640]{0:T(1024)S(1)}, f32[640]{0:T(1024)}, u32[]{:S(2)}) copy-start(f32[640]{0:T(1024)} %copy-done.61) | copy-start | bytes 7684
  615.2 37.9 %copy-start.64 = (f32[640]{0:T(1024)S(1)}, f32[640]{0:T(1024)}, u32[]{:S(2)}) copy-start(f32[640]{0:T(1024)} %copy-done.63) | copy-start | bytes 7684
  615.2 37.9 %copy-start.66 = (f32[640]{0:T(1024)S(1)}, f32[640]{0:T(1024)}, u32[]{:S(2)}) copy-start(f32[640]{0:T(1024)} %copy-done.65) | copy-start | bytes 7684
  615.3 108.0 %reduce-scatter.31.cloned.1.call-start = ((), (), s32[]{:S(2)}) async-start(), calls=%async_computation.23 | async-start | bytes 368640
  647.4 5.8 collective-permute-start.1
  649.6 108.7 %all-reduce.71.cloned.1.call-start = ((), (), s32[]{:S(2)}) async-start(), calls=%async_computation.13 | async-start | bytes 3276800 | tf_op jit(solution)/shard_map/psum | solution.py:187
  660.8 164.3 %reduce-scatter.19.cloned.1.call-start = ((), (), s32[]{:S(2)}) async-start(), calls=%async_computation.16 | async-start | bytes 737280 | tf_op jit(solution)/shard_map/reduce_scatter | solution.py:198
  669.8 220.9 %reduce-scatter.21.cloned.1.call-start = ((), (), s32[]{:S(2)}) async-start(), calls=%async_computation.17 | async-start | bytes 737280 | tf_op jit(solution)/shard_map/reduce_scatter | solution.py:199
  677.7 338.1 %reduce-scatter.23.cloned.1.call-start = ((), (), s32[]{:S(2)}) async-start(), calls=%async_computation.18 | async-start | bytes 7372800 | tf_op jit(solution)/shard_map/reduce_scatter | solution.py:201
  681.7 459.0 %reduce-scatter.17.cloned.1.call-start = ((), (), s32[]{:S(2)}) async-start(), calls=%async_computation.15 | async-start | bytes 7372800 | tf_op jit(solution)/shard_map/reduce_scatter | solution.py:195
  687.0 579.0 %reduce-scatter.15.cloned.1.call-start = ((), (), s32[]{:S(2)}) async-start(), calls=%async_computation.14 | async-start | bytes 7372800 | tf_op jit(solution)/shard_map/reduce_scatter | solution.py:194
  692.0 901.5 %reduce-scatter.25.cloned.1.call-start = ((), (), s32[]{:S(2)}) async-start(), calls=%async_computation.19 | async-start | bytes 22118400 | tf_op jit(solution)/shard_map/reduce_scatter | solution.py:203
  701.5 1219.4 %reduce-scatter.27.cloned.1.call-start = ((), (), s32[]{:S(2)}) async-start(), calls=%async_computation.20 | async-start | bytes 22118400 | tf_op jit(solution)/shard_map/reduce_scatter | solution.py:204
  710.8 1537.4 %reduce-scatter.29.cloned.1.call-start = ((), (), s32[]{:S(2)}) async-start(), calls=%async_computation.21 | async-start | bytes 22118400 | tf_op jit(solution)/shard_map/reduce_scatter | solution.py:205
  720.7 39.6 %copy-start.55 = (f32[2560]{0:T(1024)S(1)}, f32[2560]{0:T(1024)}, u32[]{:S(2)}) copy-start(f32[2560]{0:T(1024)} %get-tuple-element.241) | copy-start | bytes 30724
  800.2 1447.9 %copy-start.1 = (bf16[2560,640]{1,0:T(8,128)(2,1)S(1)}, bf16[2560,640]{1,0:T(8,128)(2,1)}, u32[]{:S(2)}) copy-start(bf16[2560,640]{1,0:T(8,128)(2,1)} %param.22) | copy-start | bytes 9830404
  (51 other events, 129.5 us)
Sparse Core Ops, SparseCore 0:
  224.1 42.5 all-reduce.66
  299.4 43.9 all-reduce.68
  345.6 47.8 all-gather.2
  615.3 28.2 reduce-scatter.12
  649.7 63.3 reduce-scatter.30
  715.3 42.9 all-reduce.70
  762.2 62.8 reduce-scatter.18
  829.0 61.6 reduce-scatter.20
  894.9 120.7 reduce-scatter.22
  1019.8 120.9 reduce-scatter.16
  1145.0 120.9 reduce-scatter.14
  1270.3 323.0 reduce-scatter.24
  1597.9 322.9 reduce-scatter.26
  1925.2 322.8 reduce-scatter.28
